TPU v7x, 128 devices: a whole 4x4x4 slice. The times are simulated.
128 devices in a mesh: batch: 8 (over y_lo, x), corpus: 16 (over z, y_hi, core).
Axes of the slice: x: 4, y: 4 (y_hi: 2, y_lo: 2; y = y_hi * 2 + y_lo), z: 4, core: 2. Of those that a mesh axis runs over, the one named last changes fastest.
Arguments:
- states: bfloat16 [8192, 4096], P('batch', 'corpus'), may hold values from -6 to 6
- norm_gain: float32 [4096], replicated, may hold values from 0.25 to 1.75
- gate_weight: bfloat16 [4096, 12288], P('batch', 'corpus'), may hold values from -0.09375 to 0.09375
- up_weight: bfloat16 [4096, 12288], P('batch', 'corpus'), may hold values from -0.09375 to 0.09375
- down_weight: bfloat16 [12288, 4096], P('corpus', 'batch'), may hold values from -0.0546875 to 0.0546875
- final_gain: float32 [4096], replicated, may hold values from 0.25 to 1.75
- hash_weight: bfloat16 [4096, 1024], replicated, may hold values from -0.75 to 0.75
- query_bits: bfloat16 [4096, 1024], replicated, may hold values from -1 to 1
- slot_map: int32 [128], replicated, may hold values from 0 to 127, each once
- query_index: int32 [4096, 100], replicated, may hold values from 0 to 127
Outputs:
- scores: float32 [4096, 100], P(('batch', 'corpus'))
Inputs may be any that keep to these rules, and one draw needn't show every extreme that they name: `slot_map`: each corpus entry is named by exactly one document.
All inputs are finite; a program needn't handle non-finite values.
Results may differ from a plain program's by a relative error of at most 0.017.
Values may be sent and summed in bfloat16 or wider, within the bound.
No kernel may reach another device: no remote copies, remote signals or barrier semaphores. Data moves between devices by JAX's collectives and lax.ppermute only.
A program may use at most 192 MiB of HBM per device.

v0:
```python
import jax
import jax.numpy as jnp
from jax import lax
from jax.sharding import PartitionSpec as P

DOC_LEN = 64
CODE = 1024
NQ = 4096


def side_by_side(arrays, axis, dim, along):
    both = jnp.concatenate(arrays, axis=along)
    whole, at, gathered = (lax.all_gather(both, axis, axis=dim, tiled=True), 0, [])
    for a in arrays:
        gathered.append(lax.slice_in_dim(whole, at, at + a.shape[along], axis=along))
        at += a.shape[along]
    return tuple(gathered)


def rms(values, gain):
    return values * lax.rsqrt(jnp.mean(values * values, axis=-1, keepdims=True) + 1e-06) * gain


def add_rows(left, piece):
    return jnp.dot(left, piece, preferred_element_type=jnp.float32)


def local(
    states,
    norm_gain,
    gate_weight,
    up_weight,
    down_weight,
    final_gain,
    hash_weight,
    query_bits,
    slot_map,
    query_index,
):
    corpus_count = lax.axis_size("corpus")
    devices = lax.axis_size("batch") * corpus_count
    flat_index = lax.axis_index("batch") * corpus_count + lax.axis_index("corpus")
    whole = lax.all_gather(states, "corpus", axis=1, tiled=True)
    normed = rms(whole.astype(jnp.float32), norm_gain).astype(jnp.bfloat16)
    pieces = side_by_side((gate_weight, up_weight), "batch", 0, 1)
    gate = add_rows(normed, pieces[0])
    up = add_rows(normed, pieces[1])
    hidden = (jax.nn.silu(gate) * up).astype(jnp.bfloat16)
    terms = jnp.dot(
        hidden,
        lax.all_gather(down_weight, "batch", axis=1, tiled=True),
        preferred_element_type=jnp.float32,
    )
    ffn = lax.psum_scatter(
        terms.astype(jnp.bfloat16), "corpus", scatter_dimension=0, tiled=True
    ).astype(jnp.float32)
    own_rows = ffn.shape[0]
    mine = lax.dynamic_slice_in_dim(whole, lax.axis_index("corpus") * own_rows, own_rows, 0)
    resid = mine.astype(jnp.float32) + ffn
    finals = rms(resid, final_gain)
    owned_docs = own_rows // DOC_LEN
    pooled = jnp.mean(finals.reshape(owned_docs, DOC_LEN, finals.shape[1]), axis=1).astype(
        jnp.bfloat16
    )
    codes = jnp.tanh(jnp.dot(pooled, hash_weight, preferred_element_type=jnp.float32)).astype(
        jnp.bfloat16
    )
    doc_total = owned_docs * devices
    scale = 1.0 / jnp.sqrt(jnp.float32(CODE))
    gathered = lax.all_gather(codes, ("batch", "corpus"), axis=0, tiled=True)
    placing = (slot_map[:, None] == jnp.arange(doc_total, dtype=jnp.int32)[None, :]).astype(
        jnp.bfloat16
    )
    corpus = jnp.einsum("ds,dc->sc", placing, gathered, preferred_element_type=jnp.float32).astype(
        jnp.bfloat16
    )
    query_rows = NQ // devices
    my_bits = lax.dynamic_slice_in_dim(query_bits, flat_index * query_rows, query_rows, 0)
    my_index = lax.dynamic_slice_in_dim(query_index, flat_index * query_rows, query_rows, 0)
    table = jnp.dot(my_bits, corpus.T, preferred_element_type=jnp.float32) * scale
    scores = jnp.take_along_axis(table, my_index, axis=1)
    return scores


def solution(mesh):
    placed = (
        P("batch", "corpus"),
        P(),
        P("batch", "corpus"),
        P("batch", "corpus"),
        P("corpus", "batch"),
        P(),
        P(),
        P(),
        P(),
        P(),
    )
    return jax.shard_map(
        local, mesh=mesh, in_specs=placed, out_specs=P(("batch", "corpus"), None), check_vma=False
    )
```

profile of v0, /device:TPU:1, one launch (start us, length us, event | category | flops | bytes accessed | tf_op | source)
XLA Modules:
  0.0 631.7 jit_solution(1051141560968313369)
XLA Ops:
  6.5 0.0 copy-start
  6.5 0.0 all-gather.5.cloned.1.call-start
  6.5 0.7 all-gather.5.cloned.1.call-update
  7.3 0.0 copy-start.3
  7.3 0.0 all-gather.7.cloned.1.call-start
  7.3 2.7 pad_maximum_fusion
  10.0 0.0 all-gather.7.cloned.1.call-update
  10.0 0.0 all-gather.9.cloned.1.call-start
  10.1 0.7 all-gather.9.cloned.1.call-update
  10.7 0.0 reduce-scatter.2.cloned.1.call-start
  10.8 79.1 %all-gather.5.cloned.1.call-done = bf16[1024,4096]{1,0:T(8,128)(2,1)} async-done(((bf16[1024,256]{1,0:T(8,128)(2,1)}), bf16[1024,4096]{1,0:T(8,128)(2,1)}) %all-gather.5.cloned.1.call-update) | async-done | bytes 8388624 | tf_op jit(solution)/shard_map/all_gather | solution.py:43
  89.9 5.1 fusion
  95.0 124.5 %all-gather.7.cloned.1.call-done = bf16[4096,1536]{1,0:T(8,128)(2,1)} async-done(((bf16[512,1536]{1,0:T(8,128)(2,1)}), bf16[4096,1536]{1,0:T(8,128)(2,1)}) %all-gather.7.cloned.1.call-update) | async-done | bytes 12582928 | tf_op jit(solution)/shard_map/all_gather | solution.py:13
  219.5 0.0 copy-done.3
  219.5 12.4 %fusion.3 = f32[1024,768]{1,0:T(8,128)} fusion(bf16[4096,1536]{1,0:T(8,128)(2,1)} %all-gather.7.cloned.1.call-done, bf16[1024,4096]{1,0:T(8,128)(2,1)} %all-gather.5.cloned.1.call-done, f32[4096]{0:T(1024)S(1)} %copy-done.3, f32[1024]{0:T(1024)S(1)} %add_rsqrt_fusion), kind=kOutput, calls=%fused_computation.7 | convolution fusion | flops 6459228160 | bytes 17846272 | tf_op jit(solution)/shard_map/dot_general | solution.py:25
  231.9 60.2 %all-gather.9.cloned.1.call-done = bf16[768,4096]{1,0:T(8,128)(2,1)} async-done(((bf16[768,512]{1,0:T(8,128)(2,1)}), bf16[768,4096]{1,0:T(8,128)(2,1)}) %all-gather.9.cloned.1.call-update) | async-done | bytes 6291472 | tf_op jit(solution)/shard_map/all_gather | solution.py:51
  292.1 26.3 %convolution_convert_fusion = bf16[1024,4096]{1,0:T(8,128)(2,1)} fusion(bf16[768,4096]{1,0:T(8,128)(2,1)} %all-gather.9.cloned.1.call-done, f32[1024,768]{1,0:T(8,128)} %fusion.3, bf16[4096,1536]{1,0:T(8,128)(2,1)} %all-gather.7.cloned.1.call-done, bf16[1024,4096]{1,0:T(8,128)(2,1)} %all-gather.5.cloned.1.call-done, f32[4096]{0:T(1024)S(1)} %copy-done.3, ...), kind=kOutput, calls=%fused_computation.6 | convolution fusion | flops 12910592000 | bytes 32526336 | tf_op jit(solution)/shard_map/dot_general | solution.py:49
  318.4 0.0 copy-start.1
  318.4 0.0 reduce-scatter.2.cloned.1.call-update
  318.4 0.0 copy-done
  318.4 0.1 constant_dynamic-slice_fusion
  318.5 0.1 copy.14
  318.6 0.1 reshape.40
  318.7 99.8 %reduce-scatter.2.cloned.1.call-done = bf16[64,4096]{1,0:T(8,128)(2,1)} async-done(((bf16[1024,4096]{1,0:T(8,128)(2,1)}), bf16[64,4096]{1,0:T(8,128)(2,1)}) %reduce-scatter.2.cloned.1.call-update) | async-done | bytes 524304 | tf_op jit(solution)/shard_map/reduce_scatter | solution.py:54
  418.5 1.5 multiply_reduce_fusion.1
  420.0 0.0 copy-done.1
  420.0 1.5 multiply_reduce_fusion
  421.5 0.0 copy-start.2
  421.5 4.6 fusion.25
  426.1 177.8 %all-gather = bf16[131072]{0:T(1024)(128)(2,1)S(1)} all-gather(bf16[1024]{0:T(1024)(128)(2,1)S(1)} %tanh_convert_fusion), channel_id=2, replica_groups=mesh['batch'=8,'corpus'=16] {'batch','corpus'}, dimensions={0}, use_global_device_ids=true | all-gather | bytes 264192 | tf_op jit(solution)/shard_map/all_gather | solution.py:70
  603.9 0.1 reshape.46
  604.1 0.0 copy-done.2
  604.1 1.3 fusion.19
  605.4 19.0 %gather_fusion = f32[3200]{0:T(1024)S(1)} fusion(f32[32,128]{1,0:T(8,128)S(1)} %fusion.19, s32[3200]{0:T(1024)S(1)} %reshape.40), kind=kCustom, calls=%fused_computation | custom fusion | bytes 51200 | tf_op jit(solution)/shard_map/jit(take_along_axis)/gather | solution.py:81
  624.4 0.1 reshape.43
  624.5 0.6 and_select_fusion
  (6 shorter events, 0.1 us)
Async XLA Ops:
  6.5 311.9 %copy-start = (s32[4096,100]{0,1:T(8,128)S(1)}, s32[4096,100]{0,1:T(8,128)}, u32[]{:S(2)}) copy-start(s32[4096,100]{0,1:T(8,128)} %param.19) | copy-start | bytes 4915204
  6.5 83.3 %all-gather.5.cloned.1.call-start = ((), (), s32[]{:S(2)}) async-start(), calls=%async_computation.1 | async-start | bytes 8912896 | tf_op jit(solution)/shard_map/all_gather | solution.py:43
  7.3 212.2 %copy-start.3 = (f32[4096]{0:T(1024)S(1)}, f32[4096]{0:T(1024)}, u32[]{:S(2)}) copy-start(f32[4096]{0:T(1024)} %param.11) | copy-start | bytes 49156
  7.3 212.2 %all-gather.7.cloned.1.call-start = ((), (), s32[]{:S(2)}) async-start(), calls=%async_computation.2 | async-start | bytes 14155776 | tf_op jit(solution)/shard_map/all_gather | solution.py:13
  10.0 282.1 %all-gather.9.cloned.1.call-start = ((), (), s32[]{:S(2)}) async-start(), calls=%async_computation.3 | async-start | bytes 7077888 | tf_op jit(solution)/shard_map/all_gather | solution.py:51
  10.7 407.8 %reduce-scatter.2.cloned.1.call-start = ((), (), s32[]{:S(2)}) async-start(), calls=%async_computation.4 | async-start | bytes 8912896 | tf_op jit(solution)/shard_map/reduce_scatter | solution.py:54
  318.4 101.6 %copy-start.1 = (f32[4096]{0:T(1024)S(1)}, f32[4096]{0:T(1024)}, u32[]{:S(2)}) copy-start(f32[4096]{0:T(1024)} %param.15) | copy-start | bytes 49156
  421.5 182.6 %copy-start.2 = (s32[128]{0:T(128)S(1)}, s32[128]{0:T(128)}, u32[]{:S(2)}) copy-start(s32[128]{0:T(128)} %param.18) | copy-start | bytes 1540
Sparse Core Ops, SparseCore 0:
  9.7 80.1 all-gather.4
  91.5 127.9 all-gather.6
  221.1 70.9 all-gather.8
  318.5 99.9 reduce-scatter.1
where the time goes:
time: 632 us
  waiting for transfers between devices  365 us (58%)
  blocking collectives  178 us (28%)
  matrix products  44.6 us (7%)
  local copies, waits for them, and re-layouts  19.5 us (3%)
  between operations  13.2 us (2%)
  other arithmetic  11.3 us (2%)
    all_gather x1, blocking collectives, local(): gathered = lax.all_gather(codes, ('batch', 'corpus'), axis=0, tiled=True)  178 us
    all_gather x1, waiting for transfers between devices, side_by_side(): lax.all_gather(both, axis, axis=dim, tiled=True)  125 us
    reduce_scatter x1, waiting for transfers between devices, local(): lax.psum_scatter(terms.astype(jnp.bfloat16), 'corpus', scatter_dimension=...  99.8 us
    all_gather x1, waiting for transfers between devices, local(): whole = lax.all_gather(states, 'corpus', axis=1, tiled=True)  79.1 us
    all_gather x1, waiting for transfers between devices, local(): lax.all_gather(down_weight, 'batch', axis=1, tiled=True)  60.2 us
    dot_general x1, matrix products, local(): jnp.dot(hidden, lax.all_gather(down_weight, 'batch', axis=1, tiled=True),...  26.3 us
    gather x3, local copies, waits for them, and re-layouts, local(): scores = jnp.take_along_axis(table, my_index, axis=1)  19.2 us
  transfers between devices with their start and end apart: 4, of which 4 were waited for; matrix products, arithmetic and copies ran while one was open for 3% of the time, Pallas kernels for 0%

commit v1 on v0

--- a/solution.py
+++ b/solution.py
@@ -1,3 +1,4 @@
+import functools
 import jax
 import jax.numpy as jnp
 from jax import lax
@@ -6,6 +7,22 @@
 DOC_LEN = 64
 CODE = 1024
 NQ = 4096
+
+
+def post_state_now(message, array_axis):
+    o_now = jnp.concatenate(
+        lax.all_to_all(
+            jnp.stack(tuple((message for _ in range(lax.axis_size("corpus"))))),
+            axis_name="corpus",
+            split_axis=0,
+            concat_axis=0,
+        ),
+        array_axis,
+    )
+    return o_now
+
+
+plan_links = functools.partial(post_state_now, array_axis=1)
 
 
 def side_by_side(arrays, axis, dim, along):
@@ -40,7 +57,7 @@
     corpus_count = lax.axis_size("corpus")
     devices = lax.axis_size("batch") * corpus_count
     flat_index = lax.axis_index("batch") * corpus_count + lax.axis_index("corpus")
-    whole = lax.all_gather(states, "corpus", axis=1, tiled=True)
+    whole = plan_links(states)
     normed = rms(whole.astype(jnp.float32), norm_gain).astype(jnp.bfloat16)
     pieces = side_by_side((gate_weight, up_weight), "batch", 0, 1)
     gate = add_rows(normed, pieces[0])

time: 632 us -> 657 us (1.040)
  blocking collectives: 178 us -> 460 us
  waiting for transfers between devices: 365 us -> 98.3 us
  local copies, waits for them, and re-layouts: 19.5 us -> 29.1 us
    all_to_all x0 -> x1, blocking collectives: none -> 282 us  [post_state_now(): lax.all_to_all(jnp.stack(tuple((message for _ in range(lax.axis_size('cor...]
    all_gather x1, waiting for transfers between devices: 125 us -> 0.02 us  [side_by_side(): lax.all_gather(both, axis, axis=dim, tiled=True)]
    all_gather x1 -> x0, waiting for transfers between devices: 79.1 us -> none  [local(): whole = lax.all_gather(states, 'corpus', axis=1, tiled=True)]
    all_gather x1, waiting for transfers between devices: 60.2 us -> 0.01 us  [local(): lax.all_gather(down_weight, 'batch', axis=1, tiled=True)]
    reshape x0 -> x1, local copies, waits for them, and re-layouts: none -> 7.75 us  [post_state_now(): jnp.concatenate(lax.all_to_all(jnp.stack(tuple((message for _ in range(la...]
  transfers between devices with their start and end apart: 4 -> 3, of which waited for: 4 -> 1; matrix products, arithmetic and copies ran while one was open for 3% -> 4% of each run, Pallas kernels for 0% -> 0%
where the time goes in v1:
time: 657 us; the launch traced here: 656 us
  blocking collectives  460 us (70%)
  waiting for transfers between devices  98.3 us (15%)
  matrix products  44.6 us (7%)
  local copies, waits for them, and re-layouts  29.1 us (4%)
  between operations  13.2 us (2%)
  other arithmetic  11.4 us (2%)
    all_to_all x1, blocking collectives, post_state_now(): lax.all_to_all(jnp.stack(tuple((message for _ in range(lax.axis_size('cor...  282 us
    all_gather x1, blocking collectives, local(): gathered = lax.all_gather(codes, ('batch', 'corpus'), axis=0, tiled=True)  178 us
    reduce_scatter x1, waiting for transfers between devices, local(): lax.psum_scatter(terms.astype(jnp.bfloat16), 'corpus', scatter_dimension=...  97.5 us
    dot_general x1, matrix products, local(): jnp.dot(hidden, lax.all_gather(down_weight, 'batch', axis=1, tiled=True),...  26.3 us
    gather x3, local copies, waits for them, and re-layouts, local(): scores = jnp.take_along_axis(table, my_index, axis=1)  19.2 us
  transfers between devices with their start and end apart: 3, of which 1 were waited for; matrix products, arithmetic and copies ran while one was open for 4% of the time, Pallas kernels for 0%

profile of v1, /device:TPU:1, one launch (start us, length us, event | category | flops | bytes accessed | tf_op | source)
XLA Modules:
  0.0 656.3 jit_solution(8743944974505867459)
XLA Ops:
  6.5 0.0 copy-start
  6.5 0.0 all-gather.4.cloned.1.call-start
  6.5 2.7 pad_maximum_fusion
  9.3 0.0 all-gather.4.cloned.1.call-update
  9.3 0.0 all-gather.6.cloned.1.call-start
  9.4 0.7 all-gather.6.cloned.1.call-update
  10.1 0.0 reduce-scatter.2.cloned.1.call-start
  10.1 1.8 stack.2
  12.0 281.7 %all_to_all.5 = bf16[16,1024,256]{2,1,0:T(8,128)(2,1)} all-to-all(bf16[16,1024,256]{2,1,0:T(8,128)(2,1)S(1)} %stack.2), channel_id=1, replica_groups=mesh['batch'=8,'corpus'=16] {'corpus'}, dimensions={0} | all-to-all | bytes 16777216 | tf_op jit(solution)/shard_map/all_to_all | solution.py:14
  293.7 7.7 %copy.16 = bf16[16,128,8,256]{3,2,0,1:T(8,128)(2,1)} copy(bf16[16,128,8,256]{3,2,1,0:T(8,128)(2,1)} %bitcast.13) | data formatting | bytes 16777216 | tf_op jit(solution)/shard_map/reshape | solution.py:13
  301.4 0.0 copy-start.3
  301.4 5.1 multiply_reduce_fusion
  306.5 0.0 all-gather.4.cloned.1.call-done
  306.6 0.0 copy-done.3
  306.6 12.4 %fusion = f32[1024,768]{1,0:T(8,128)} fusion(bf16[4096,1536]{1,0:T(8,128)(2,1)} %all-gather.4.cloned.1.call-done, bf16[1024,4096]{1,0:T(8,128)(2,1)} %bitcast.14, f32[4096]{0:T(1024)S(1)} %copy-done.3, f32[1024]{0:T(1024)S(1)} %add_rsqrt_fusion), kind=kOutput, calls=%fused_computation.4 | convolution fusion | flops 6459228160 | bytes 17846272 | tf_op jit(solution)/shard_map/dot_general | solution.py:42
  319.0 0.0 all-gather.6.cloned.1.call-done
  319.0 26.3 %convolution_convert_fusion = bf16[1024,4096]{1,0:T(8,128)(2,1)} fusion(bf16[768,4096]{1,0:T(8,128)(2,1)} %all-gather.6.cloned.1.call-done, f32[1024,768]{1,0:T(8,128)} %fusion, bf16[4096,1536]{1,0:T(8,128)(2,1)} %all-gather.4.cloned.1.call-done, bf16[1024,4096]{1,0:T(8,128)(2,1)} %bitcast.15, f32[4096]{0:T(1024)S(1)} %copy-done.3, f32[1024]{0:T(1024)S(1)} %add_rsqrt_fusion), kind=kOutput, calls=%fused_computation.3 | convolution fusion | flops 12910592000 | bytes 32526336 | tf_op jit(solution)/shard_map/dot_general | solution.py:66
  345.3 0.0 copy-start.1
  345.3 0.0 reduce-scatter.2.cloned.1.call-update
  345.3 0.0 copy-done
  345.3 0.1 constant_dynamic-slice_fusion
  345.4 0.1 copy.15
  345.5 0.1 reshape.50
  345.6 97.5 %reduce-scatter.2.cloned.1.call-done = bf16[64,4096]{1,0:T(8,128)(2,1)} async-done(((bf16[1024,4096]{1,0:T(8,128)(2,1)}), bf16[64,4096]{1,0:T(8,128)(2,1)}) %reduce-scatter.2.cloned.1.call-update) | async-done | bytes 524304 | tf_op jit(solution)/shard_map/reduce_scatter | solution.py:71
  443.1 1.5 multiply_reduce_fusion.2
  444.6 0.0 copy-done.1
  444.6 1.5 multiply_reduce_fusion.1
  446.1 0.0 copy-start.2
  446.1 4.6 fusion.16
  450.7 177.8 %all-gather = bf16[131072]{0:T(1024)(128)(2,1)S(1)} all-gather(bf16[1024]{0:T(1024)(128)(2,1)S(1)} %tanh_convert_fusion), channel_id=2, replica_groups=mesh['batch'=8,'corpus'=16] {'batch','corpus'}, dimensions={0}, use_global_device_ids=true | all-gather | bytes 264192 | tf_op jit(solution)/shard_map/all_gather | solution.py:87
  628.5 0.1 reshape.56
  628.7 0.0 copy-done.2
  628.7 1.3 fusion.10
  630.0 19.0 %gather_fusion = f32[3200]{0:T(1024)S(1)} fusion(f32[32,128]{1,0:T(8,128)S(1)} %fusion.10, s32[3200]{0:T(1024)S(1)} %reshape.50), kind=kCustom, calls=%fused_computation | custom fusion | bytes 51200 | tf_op jit(solution)/shard_map/jit(take_along_axis)/gather | solution.py:98
  649.0 0.1 reshape.53
  649.1 0.6 and_select_fusion
  (6 shorter events, 0.1 us)
Async XLA Ops:
  6.5 338.8 %copy-start = (s32[4096,100]{0,1:T(8,128)S(1)}, s32[4096,100]{0,1:T(8,128)}, u32[]{:S(2)}) copy-start(s32[4096,100]{0,1:T(8,128)} %param.19) | copy-start | bytes 4915204
  6.5 300.0 %all-gather.4.cloned.1.call-start = ((), (), s32[]{:S(2)}) async-start(), calls=%async_computation.2 | async-start | bytes 14155776 | tf_op jit(solution)/shard_map/all_gather | solution.py:30
  9.3 309.7 %all-gather.6.cloned.1.call-start = ((), (), s32[]{:S(2)}) async-start(), calls=%async_computation.3 | async-start | bytes 7077888 | tf_op jit(solution)/shard_map/all_gather | solution.py:68
  10.1 433.1 %reduce-scatter.2.cloned.1.call-start = ((), (), s32[]{:S(2)}) async-start(), calls=%async_computation.4 | async-start | bytes 8912896 | tf_op jit(solution)/shard_map/reduce_scatter | solution.py:71
  301.4 5.1 copy-start.3
  345.3 99.3 %copy-start.1 = (f32[4096]{0:T(1024)S(1)}, f32[4096]{0:T(1024)}, u32[]{:S(2)}) copy-start(f32[4096]{0:T(1024)} %param.15) | copy-start | bytes 49156
  446.1 182.6 %copy-start.2 = (s32[128]{0:T(128)S(1)}, s32[128]{0:T(128)}, u32[]{:S(2)}) copy-start(s32[128]{0:T(128)} %param.18) | copy-start | bytes 1540
Sparse Core Ops, SparseCore 0:
  9.4 134.2 all-gather.3
  145.3 70.9 all-gather.5
  345.4 97.6 reduce-scatter.1
